TPU v7x, 32 devices: a whole 2x2x4 slice. The times are simulated.
32 devices in a mesh: sec: 8 (over z, y), tile: 4 (over x, core).
Axes of the slice: x: 2, y: 2, z: 4, core: 2. Of those that a mesh axis runs over, the one named last changes fastest.
Arguments:
- image: bfloat16 [8, 1024, 1024], P('sec', 'tile'), may hold values from -6 to 6
- weight: bfloat16 [8, 1024, 1024], P('sec', 'tile'), may hold values from 0.25 to 4
- lens_filter_taps: float32 [8, 4, 25], P('sec', 'tile'), may hold values from -2 to 2
- block_src: int32 [8, 4, 4, 2], P('sec', 'tile'), may hold values from 0 to 15
- block_dst: int32 [8, 4, 4, 2], P('sec', None, 'tile'), may hold values from 0 to 3, as said below
- valid_count: int32 [8, 4, 4], P('sec', 'tile'), may hold values from 1 to 2, as said below
- anchor: bfloat16 [16, 128, 128], P('tile'), may hold values from -6 to 6
Outputs:
- correlation: float32 [8, 32, 128, 128], P('sec', 'tile')
Inputs may be any that keep to these rules, and one draw needn't show every extreme that they name: `block_dst`: every block of every strip receives at least one live slot. `valid_count`: in every section some strip receives 2 live slots from every tile; block_src and block_dst are 0 in slots at or beyond the valid count.
All inputs are finite; a program needn't handle non-finite values.
Results may differ from a plain program's by a relative error of at most 0.02.
Values may be sent and summed in bfloat16 or wider, within the bound.
A program may use at most 64 MiB of HBM per device.

v0:
```python
import functools
import math

import jax
import jax.numpy as jnp
import numpy as np
from jax import lax
from jax.experimental import pallas as pl
from jax.experimental.pallas import tpu as pltpu
from jax.sharding import PartitionSpec as P

MESH = pl.DeviceIdType.MESH
EDGE = 16
LANES = 128


def repeat(count, step):
    if count <= 4:
        for i in range(count):
            step(i)
    else:
        pl.loop(0, count)(step)


def dft_tables(size):
    positions = np.arange(size)
    angle = (positions[:, None] * positions[None, :] % size) * (2.0 * math.pi / size)
    cosine, sine = np.cos(angle), np.sin(angle)
    inverse_right = np.block([[cosine, sine], [-sine, cosine]])
    forward_left = np.block([[cosine, -sine], [-sine, -cosine]])
    return jnp.asarray(np.concatenate([inverse_right, forward_left], 0), jnp.bfloat16)


def lens(rows, taps, first, count):
    left, middle, right = rows
    lane = lax.broadcasted_iota(jnp.int32, middle.shape, 1)
    shifted = []
    for off in range(-2, 3):
        if off == 0:
            shifted.append(middle)
        elif off > 0:
            mixed = jnp.where(lane < off, right, middle)
            shifted.append(pltpu.roll(mixed, LANES - off, 1))
        else:
            mixed = jnp.where(lane >= LANES + off, left, middle)
            shifted.append(pltpu.roll(mixed, -off, 1))
    total = None
    n = middle.shape[0]
    for a in range(5):
        part = taps[5 * a] * shifted[0]
        for b in range(1, 5):
            part = part + taps[5 * a + b] * shifted[b]
        if a != 2:
            part = pltpu.roll(part, (2 - a) % n, 0)
        part = part[first : first + count]
        total = part if total is None else total + part
    return total


def kernel(
    sections,
    tiles,
    image,
    weight,
    anchor,
    tables,
    taps_any,
    src_any,
    dst_any,
    valid_any,
    out,
    taps_ref,
    src_ref,
    dst_ref,
    valid_ref,
    img,
    wgt,
    halo,
    out_mid,
    out_edge,
    in_mid,
    in_edge,
    strip_mid,
    strip_edge,
    pre_mid,
    pre_edge,
    spec,
    tab,
    load_sem,
    halo_send,
    halo_recv,
    mid_send,
    mid_recv,
    edge_send,
    edge_recv,
    strip_send,
    strip_recv,
    anchor_send,
):
    sec = lax.axis_index("sec")
    me = lax.axis_index("tile")
    th, tw = image.shape[1:]
    side = wgt.shape[1]
    blocks = strip_mid.shape[0] - 1
    cap = in_mid.shape[1]
    across, down = tw // side, th // side
    padded = across + 2
    mid = side - 2 * EDGE

    barrier = pltpu.get_barrier_semaphore()

    def greet(target):
        pl.semaphore_signal(barrier, inc=1, device_id=target, device_id_type=MESH)

    for k in range(1, tiles):
        greet((sec, lax.rem(me + k, tiles)))
    has_next, has_prev = sec < sections - 1, sec > 0
    not_first, not_last = me > 0, me < tiles - 1

    @pl.when(has_next)
    def _():
        greet((sec + 1, me))

    @pl.when(has_next & not_first)
    def _():
        greet((sec + 1, me - 1))

    @pl.when(has_prev)
    def _():
        greet((sec - 1, me))

    @pl.when(has_prev & not_last)
    def _():
        greet((sec - 1, me + 1))

    loads = []
    for source, ref in (
        (taps_any, taps_ref),
        (src_any, src_ref),
        (dst_any, dst_ref),
        (valid_any, valid_ref),
    ):
        loads.append(pltpu.make_async_copy(source, ref, load_sem.at[len(loads)]))
    for r in range(down):
        low, high = max(0, r * side - EDGE), min(th, (r + 1) * side + EDGE)
        place = low - (r * side - EDGE)
        for c in range(across):
            columns = pl.ds(c * side, side)
            loads.append(
                pltpu.make_async_copy(
                    image.at[0, pl.ds(low, high - low), columns],
                    img.at[r * padded + c + 1, pl.ds(place, high - low)],
                    load_sem.at[len(loads)],
                )
            )
            loads.append(
                pltpu.make_async_copy(
                    weight.at[0, pl.ds(r * side, side), columns],
                    wgt.at[r * across + c],
                    load_sem.at[len(loads)],
                )
            )
    table_load = pltpu.make_async_copy(tables, tab, load_sem.at[len(loads)])
    for load in loads:
        load.start()
    table_load.start()

    inner, upper, lower = pl.ds(EDGE, mid), pl.ds(0, EDGE), pl.ds(side - EDGE, EDGE)
    rim_at = 2 * blocks

    def anchor_load(j):
        for rows, ref, at in (
            (inner, pre_mid.at[j], 2 * j),
            (upper, pre_edge.at[j, pl.ds(0, EDGE)], 2 * j + 1),
            (lower, pre_edge.at[j, pl.ds(EDGE, EDGE)], 2 * j + 1),
        ):
            pltpu.make_async_copy(anchor.at[j, rows], ref, strip_recv.at[at]).start()

    @pl.when(sec == 0)
    def _():
        repeat(blocks, anchor_load)

    zeros = jnp.zeros(img.shape[1:], img.dtype)
    for r in range(down):
        img[r * padded] = zeros
        img[(r + 1) * padded - 1] = zeros

    @pl.when(me == 0)
    def _():
        for c in range(across):
            img[c + 1, :EDGE] = zeros[:EDGE]

    @pl.when(me == tiles - 1)
    def _():
        for c in range(across):
            img[(down - 1) * padded + c + 1, EDGE + side :] = zeros[:EDGE]
        for ref in (strip_mid, strip_edge, pre_mid, pre_edge):
            ref[blocks] = jnp.zeros(ref.shape[1:], ref.dtype)

    def remote(src, dst, send, recv, target):
        return pltpu.make_async_remote_copy(
            src_ref=src,
            dst_ref=dst,
            send_sem=send,
            recv_sem=recv,
            device_id=target,
            device_id_type=MESH,
        )

    halo_down = remote(
        image.at[0, pl.ds(th - EDGE, EDGE)],
        halo.at[0],
        halo_send.at[0],
        halo_recv.at[0],
        (sec, lax.rem(me + 1, tiles)),
    )
    halo_up = remote(
        image.at[0, pl.ds(0, EDGE)],
        halo.at[1],
        halo_send.at[1],
        halo_recv.at[1],
        (sec, lax.rem(me + tiles - 1, tiles)),
    )
    before_me = lax.rem(me + tiles - 1, tiles)
    next_sec = lax.rem(sec + 1, sections)
    anchor_rims = [
        remote(anchor.at[0, rows], ref, anchor_send.at[n], strip_recv.at[at], (sec, before_me))
        for n, (rows, ref, at) in enumerate(
            (
                (inner, pre_mid.at[blocks], rim_at),
                (upper, pre_edge.at[blocks, pl.ds(0, EDGE)], rim_at + 1),
                (lower, pre_edge.at[blocks, pl.ds(EDGE, EDGE)], rim_at + 1),
            )
        )
    ]
    parts = ((strip_mid, pre_mid), (strip_edge, pre_edge))

    def onward(part, j):
        strip, pre = parts[part]
        at = 2 * j + part
        return remote(strip.at[j], pre.at[j], strip_send.at[at], strip_recv.at[at], (next_sec, me))

    def onward_rim(part):
        strip, pre = parts[part]
        at = rim_at + part
        return remote(
            strip.at[0], pre.at[blocks], strip_send.at[at], strip_recv.at[at], (next_sec, before_me)
        )

    def own_rim(part):
        strip, _ = parts[part]
        at = rim_at + 2 + part
        return remote(
            strip.at[0], strip.at[blocks], strip_send.at[at], strip_recv.at[at], (sec, before_me)
        )

    def start_rims(part):
        @pl.when(has_next & not_first)
        def _():
            onward_rim(part).start()

        @pl.when(not_first)
        def _():
            own_rim(part).start()

    ahead = 1

    for load in loads:
        load.wait()

    taps = [taps_ref[0, 0, k] for k in range(25)]
    chips = tiles // 2

    def owner(k):
        chip = lax.rem(me // 2 + 1 + k // 2, chips)
        return chip * 2 + lax.rem(me + 1 + k, 2)

    def picked(target, slot, first, count):
        source = src_ref[0, 0, slot, target]
        place = source + 2 * lax.div(source, across)
        rows = [
            img[place + k, first : first + count + 2 * EDGE].astype(jnp.float32) for k in range(3)
        ]
        rows = [part[EDGE - 8 : EDGE + count + 8] for part in rows]
        corrected = lens(rows, taps, 8, count)
        factor = wgt[source, first : first + count].astype(jnp.float32)
        live = jnp.clip(valid_ref[0, 0, target] - slot, 0, 1).astype(jnp.float32)
        return (corrected * factor * live).astype(jnp.bfloat16)

    def mid_copy(k):
        target = owner(k)
        return remote(
            out_mid.at[target], in_mid.at[me], mid_send.at[target], mid_recv.at[me], (sec, target)
        )

    def edge_copy(k):
        target = owner(k)
        return remote(
            out_edge.at[target],
            in_edge.at[me],
            edge_send.at[target],
            edge_recv.at[me],
            (sec, target),
        )

    def fill_mid(k, ref, place):
        for slot in range(cap):
            for piece in range(0, mid, 32):
                ref[place, slot, piece : piece + 32] = picked(owner(k), slot, EDGE + piece, 32)

    def fill_edge(k, ref, place):
        for slot in range(cap):
            ref[place, slot, :EDGE] = picked(owner(k), slot, 0, EDGE)
            ref[place, slot, EDGE:] = picked(owner(k), slot, side - EDGE, EDGE)

    def send_mid(k):
        fill_mid(k, out_mid, owner(k))
        mid_copy(k).start()

    fill_mid(0, out_mid, owner(0))
    after, before = has_next.astype(jnp.int32), has_prev.astype(jnp.int32)
    peers = after * (1 + not_first.astype(jnp.int32)) + before * (1 + not_last.astype(jnp.int32))
    pl.semaphore_wait(barrier, tiles - 1 + peers)

    @pl.when(not_last)
    def _():
        halo_down.start()

    @pl.when(not_first)
    def _():
        halo_up.start()

    @pl.when((sec == 0) & not_first)
    def _():
        for copy in anchor_rims:
            copy.start()

    mid_copy(0).start()
    pl.loop(1, tiles - 1)(send_mid)
    fill_mid(tiles - 1, in_mid, me)

    @pl.when(not_first)
    def _():
        halo_down.wait_recv()
        for c in range(across):
            img[c + 1, :EDGE] = halo[0, :, c * side : (c + 1) * side]

    @pl.when(not_last)
    def _():
        halo_up.wait_recv()
        for c in range(across):
            img[(down - 1) * padded + c + 1, EDGE + side :] = halo[
                1, :, c * side : (c + 1) * side
            ]

    def send_edge(k):
        fill_edge(k, out_edge, owner(k))
        edge_copy(k).start()

    pl.loop(0, tiles - 1)(send_edge)
    fill_edge(tiles - 1, in_edge, me)

    def summed(ref, start, count):
        totals = [None] * blocks
        for t in range(tiles):
            for slot in range(cap):
                value = ref[t, slot, pl.ds(start, count)].astype(jnp.float32)
                place = dst_ref[0, 0, slot, t]
                for j in range(blocks):
                    term = value * (1 - jnp.minimum(jnp.abs(place - j), 1)).astype(jnp.float32)
                    totals[j] = term if totals[j] is None else totals[j] + term
        return [total.astype(jnp.bfloat16) for total in totals]

    def arrive(copy_of):
        def step(k):
            source = owner(k)
            copy_of(k, source).wait_recv()

        return step

    def mid_from(k, source):
        return remote(
            out_mid.at[source], in_mid.at[source], mid_send.at[source], mid_recv.at[source], (sec, source)
        )

    def edge_from(k, source):
        return remote(
            out_edge.at[source], in_edge.at[source], edge_send.at[source], edge_recv.at[source], (sec, source)
        )

    repeat(tiles - 1, arrive(mid_from))
    for piece in range(0, mid, 32):
        for j, value in enumerate(summed(in_mid, piece, 32)):
            strip_mid[j, piece : piece + 32] = value
    start_rims(0)

    @pl.when(has_next)
    def _():
        for j in range(ahead):
            onward(0, blocks - 1 - j).start()

    repeat(tiles - 1, arrive(edge_from))
    for j, value in enumerate(summed(in_edge, 0, 2 * EDGE)):
        strip_edge[j] = value
    start_rims(1)

    @pl.when(has_next)
    def _():
        for j in range(ahead):
            onward(1, blocks - 1 - j).start()

        def later(k):
            j = blocks - 1 - ahead - k
            onward(0, j).start()
            onward(1, j).start()

        repeat(blocks - ahead, later)


    table_load.wait()
    right_table = tab.at[pl.ds(0, 2 * side)]
    left_table = tab.at[pl.ds(2 * side, 2 * side)]

    def whole(mid_ref, edge_ref, m):
        edge = edge_ref[m]
        return jnp.concatenate([edge[:EDGE], mid_ref[m], edge[EDGE:]], 0)

    def spectra(mid_ref, edge_ref, m):
        block, after = whole(mid_ref, edge_ref, m), whole(mid_ref, edge_ref, m + 1)
        lane = lax.broadcasted_iota(jnp.int32, block.shape, 1)
        shifted = jnp.where(
            lane < side // 2, after.astype(jnp.float32), block.astype(jnp.float32)
        ).astype(block.dtype)
        windows = jnp.concatenate([block, shifted], 0)
        right = jnp.dot(
            windows, right_table[:side], preferred_element_type=jnp.float32
        ).astype(jnp.bfloat16)
        stacked = jnp.concatenate(
            [
                jnp.concatenate([right[:side, :side], right[:side, side:]], 0),
                jnp.concatenate([right[side:, :side], right[side:, side:]], 0),
            ],
            1,
        )
        return jnp.dot(left_table[...], stacked, preferred_element_type=jnp.float32)

    def keep(m):
        spec[m] = spectra(strip_mid, strip_edge, m)

    repeat(blocks - 1, keep)

    @pl.when(not_last)
    def _():
        own_rim(0).wait_recv()
        own_rim(1).wait_recv()

    keep(blocks - 1)

    @pl.when(not_last)
    def _():
        onward_rim(0).wait_recv()
        onward_rim(1).wait_recv()

    def correlate(k):
        m = blocks - 1 - k
        onward(0, m).wait_recv()
        onward(1, m).wait_recv()
        earlier = spectra(pre_mid, pre_edge, m)
        current = spec[m]
        cur_re, cur_im = current[:side], current[side:]
        pre_re, pre_im = earlier[:side], earlier[side:]
        cross_re = cur_re * pre_re + cur_im * pre_im
        cross_im = cur_im * pre_re - cur_re * pre_im
        magnitude = jnp.sqrt(cross_re * cross_re + cross_im * cross_im)
        whitened = []
        for half in range(2):
            cols = slice(half * side, (half + 1) * side)
            mag = magnitude[:, cols]
            mean = jnp.sum(mag) * (1.0 / (side * side))
            scale = (1.0 / side) / (mag + (0.1 * mean + 1e-06))
            whitened.append(
                jnp.concatenate([cross_re[:, cols] * scale, cross_im[:, cols] * scale], 1)
            )
        whitened = jnp.concatenate(whitened, 0).astype(jnp.bfloat16)
        rows = jnp.dot(
            whitened, right_table[...], preferred_element_type=jnp.float32
        ).astype(jnp.bfloat16)
        stacked = jnp.concatenate(
            [
                jnp.concatenate([rows[:side, :side], rows[:side, side:]], 0),
                jnp.concatenate([rows[side:, :side], rows[side:, side:]], 0),
            ],
            1,
        )
        result = jnp.dot(left_table[:side], stacked, preferred_element_type=jnp.float32)
        out[0, 2 * m] = result[:, :side]
        out[0, 2 * m + 1] = result[:, side:]

    repeat(blocks, correlate)

    @pl.when(not_last)
    def _():
        halo_down.wait_send()

    @pl.when(not_first)
    def _():
        halo_up.wait_send()
        own_rim(0).wait_send()
        own_rim(1).wait_send()

    @pl.when((sec == 0) & not_first)
    def _():
        for copy in anchor_rims:
            copy.wait_send()

    @pl.when(has_next)
    def _():
        def gone(j):
            onward(0, j).wait_send()
            onward(1, j).wait_send()

        repeat(blocks, gone)

    @pl.when(has_next & not_first)
    def _():
        onward_rim(0).wait_send()
        onward_rim(1).wait_send()

    def left_here(k):
        mid_copy(k).wait_send()
        edge_copy(k).wait_send()

    repeat(tiles - 1, left_here)


def solution(mesh):
    sections, tiles = mesh.shape["sec"], mesh.shape["tile"]

    def body(image, weight, lens_filter_taps, block_src, block_dst, valid_count, anchor):
        th, tw = image.shape[1:]
        blocks, side = anchor.shape[:2]
        cap = block_src.shape[-1]
        anywhere = pl.BlockSpec(memory_space=pl.ANY)
        bf16 = jnp.bfloat16
        dma = pltpu.SemaphoreType.DMA
        mid = side - 2 * EDGE
        across, down = tw // side, th // side
        return pl.pallas_call(
            functools.partial(kernel, sections, tiles),
            out_shape=pltpu.VMEM((1, 2 * blocks, side, side), jnp.float32),
            in_specs=[anywhere] * 8,
            out_specs=pl.BlockSpec(memory_space=pltpu.VMEM),
            scratch_shapes=[
                pltpu.SMEM(lens_filter_taps.shape, jnp.float32),
                pltpu.SMEM((1, 1, cap, tiles), jnp.int32),
                pltpu.SMEM((1, 1, cap, tiles), jnp.int32),
                pltpu.SMEM(valid_count.shape, jnp.int32),
                pltpu.VMEM((down * (across + 2), side + 2 * EDGE, side), bf16),
                pltpu.VMEM((down * across, side, side), bf16),
                pltpu.VMEM((2, EDGE, tw), bf16),
                pltpu.VMEM((tiles, cap, mid, side), bf16),
                pltpu.VMEM((tiles, cap, 2 * EDGE, side), bf16),
                pltpu.VMEM((tiles, cap, mid, side), bf16),
                pltpu.VMEM((tiles, cap, 2 * EDGE, side), bf16),
                pltpu.VMEM((blocks + 1, mid, side), bf16),
                pltpu.VMEM((blocks + 1, 2 * EDGE, side), bf16),
                pltpu.VMEM((blocks + 1, mid, side), bf16),
                pltpu.VMEM((blocks + 1, 2 * EDGE, side), bf16),
                pltpu.VMEM((blocks, 2 * side, 2 * side), jnp.float32),
                pltpu.VMEM((4 * side, 2 * side), bf16),
                dma((2 * down * across + 5,)),
                dma((2,)),
                dma((2,)),
                dma((tiles,)),
                dma((tiles,)),
                dma((tiles,)),
                dma((tiles,)),
                dma((2 * blocks + 4,)),
                dma((2 * blocks + 4,)),
                dma((3,)),
            ],
            compiler_params=pltpu.CompilerParams(collective_id=0, has_side_effects=True),
        )(
            image,
            weight,
            anchor,
            dft_tables(side),
            lens_filter_taps,
            block_src.transpose(0, 1, 3, 2),
            block_dst.transpose(0, 2, 3, 1),
            valid_count,
        )

    in_specs = (
        P("sec", "tile", None),
        P("sec", "tile", None),
        P("sec", "tile", None),
        P("sec", "tile", None, None),
        P("sec", None, "tile", None),
        P("sec", "tile", None),
        P("tile", None, None),
    )
    out_specs = P("sec", "tile", None, None)
    return jax.shard_map(body, mesh=mesh, in_specs=in_specs, out_specs=out_specs, check_vma=False)
```

profile of v0, /device:TPU:1, one launch (start us, length us, event | category | flops | bytes accessed | tf_op | source)
XLA Modules:
  0.0 16.6 jit_solution(11788388359290007282)
XLA Ops:
  0.0 15.8 %shard_map.82 = f32[1,8,128,128]{3,2,1,0:T(8,128)S(1)} custom-call(bf16[1,256,1024]{2,1,0:T(8,128)(2,1)} %image.1, bf16[1,256,1024]{2,1,0:T(8,128)(2,1)} %weight.1, bf16[4,128,128]{2,1,0:T(8,128)(2,1)} %anchor.1, bf16[512,256]{1,0:T(8,128)(2,1)} %constant.2.clone.tables, f32[1,1,25]{2,1,0:T(1,128)} %taps_any.1, s32[1,1,2,4]{3,2,1,0:T(2,128)} %bitcast.2, ...), custom_call_target="tpu_custom_call" | custom-call | tf_op jit(solution)/shard_map/pallas_call | solution.py:548
  15.9 0.8 %copy.10 = f32[1,8,128,128]{3,2,1,0:T(8,128)} copy(f32[1,8,128,128]{3,2,1,0:T(8,128)S(1)} %shard_map.82) | data formatting | bytes 1048576
where the time goes:
time: 16.8 us; the launch traced here: 16.6 us
  Pallas kernels  15.8 us (94%)
  local copies, waits for them, and re-layouts  0.8 us (5%)
    pallas_call x1, Pallas kernels, body(): pl.pallas_call(functools.partial(kernel, sections, tiles), out_shape=pltp...  15.8 us
    unnamed x1, local copies, waits for them, and re-layouts  0.8 us

commit v1 on v0

v1 whole, which is shorter than its diff:
```python
import functools
import math

import jax
import jax.numpy as jnp
import numpy as np
from jax import lax
from jax.experimental import pallas as pl
from jax.experimental.pallas import tpu as pltpu
from jax.sharding import PartitionSpec as P

MESH = pl.DeviceIdType.MESH
EDGE = 16
HALO = 8
CHUNK = 32
LANES = 128


def repeat(count, step):
    if count <= 4:
        for i in range(count):
            step(i)
    else:
        pl.loop(0, count)(step)


def dft_tables(size):
    half = size // 2 + 8
    positions = np.arange(size)
    angle = (positions[:, None] * positions[None, :] % size) * (2.0 * math.pi / size)
    cosine, sine = np.cos(angle), np.sin(angle)
    inverse_right = np.block([[cosine, sine], [-sine, cosine]])
    kept = np.arange(half) <= size // 2
    twice = np.where((np.arange(half) == 0) | (np.arange(half) == size // 2), 1.0, 2.0) * kept
    upper_cos, upper_sin = cosine[:half] * kept[:, None], sine[:half] * kept[:, None]
    forward_left = np.block([[upper_cos, -upper_sin], [-upper_sin, -upper_cos]])
    inverse_left = np.zeros((size, 2 * size))
    inverse_left[:, :half] = cosine[:, :half] * twice / size
    inverse_left[:, half : 2 * half] = -sine[:, :half] * twice / size
    return jnp.asarray(np.concatenate([inverse_right, forward_left, inverse_left], 0), jnp.bfloat16)


def lens(rows, taps, first, count):
    left, middle, right = rows
    lane = lax.broadcasted_iota(jnp.int32, middle.shape, 1)
    shifted = []
    for off in range(-2, 3):
        if off == 0:
            shifted.append(middle)
        elif off > 0:
            mixed = jnp.where(lane < off, right, middle)
            shifted.append(pltpu.roll(mixed, LANES - off, 1))
        else:
            mixed = jnp.where(lane >= LANES + off, left, middle)
            shifted.append(pltpu.roll(mixed, -off, 1))
    total = None
    n = middle.shape[0]
    for a in range(5):
        part = taps[5 * a] * shifted[0]
        for b in range(1, 5):
            part = part + taps[5 * a + b] * shifted[b]
        if a != 2:
            part = pltpu.roll(part, (2 - a) % n, 0)
        part = part[first : first + count]
        total = part if total is None else total + part
    return total


def shifts(left, middle, right):
    lane = lax.broadcasted_iota(jnp.int32, middle.shape, 1)
    shifted = []
    for off in range(-2, 3):
        if off == 0:
            shifted.append(middle)
        elif off > 0:
            shifted.append(pltpu.roll(jnp.where(lane < off, right, middle), LANES - off, 1))
        else:
            shifted.append(pltpu.roll(jnp.where(lane >= LANES + off, left, middle), -off, 1))
    return shifted


def kernel(
    sections,
    tiles,
    image,
    weight,
    anchor,
    tables,
    taps_any,
    src_any,
    dst_any,
    valid_any,
    out,
    taps_ref,
    src_ref,
    dst_ref,
    valid_ref,
    img,
    wgt,
    halo,
    cor,
    out_buf,
    in_buf,
    out_cor,
    in_cor,
    strip,
    pre,
    strip_cor,
    pre_cor,
    rim_out,
    rim_own,
    rim_pre,
    spec,
    tab,
    load_sem,
    halo_send,
    halo_recv,
    block_send,
    block_recv,
    cor_send,
    cor_recv,
    strip_send,
    strip_recv,
    rim_send,
    rim_recv,
    next_send,
    next_recv,
):
    sec = lax.axis_index("sec")
    me = lax.axis_index("tile")
    th, tw = image.shape[1:]
    side = wgt.shape[1]
    chunks, blocks = strip.shape[0], strip.shape[1] - 1
    cap = in_buf.shape[2]
    across, down = tw // side, th // side
    padded = across + 2
    half = side // 2 + 8
    pairs = chunks // 2

    barrier = pltpu.get_barrier_semaphore()

    def greet(target):
        pl.semaphore_signal(barrier, inc=1, device_id=target, device_id_type=MESH)

    for k in range(1, tiles):
        greet((sec, lax.rem(me + k, tiles)))
    has_next, has_prev = sec < sections - 1, sec > 0
    not_first, not_last = me > 0, me < tiles - 1

    @pl.when(has_next)
    def _():
        greet((sec + 1, me))

    @pl.when(has_next & not_first)
    def _():
        greet((sec + 1, me - 1))

    @pl.when(has_prev)
    def _():
        greet((sec - 1, me))

    @pl.when(has_prev & not_last)
    def _():
        greet((sec - 1, me + 1))

    loads = []
    for source, ref in (
        (taps_any, taps_ref),
        (src_any, src_ref),
        (dst_any, dst_ref),
        (valid_any, valid_ref),
    ):
        loads.append(pltpu.make_async_copy(source, ref, load_sem.at[len(loads)]))
    for r in range(down):
        low, high = max(0, r * side - EDGE), min(th, (r + 1) * side + EDGE)
        place = low - (r * side - EDGE)
        for c in range(across):
            columns = pl.ds(c * side, side)
            loads.append(
                pltpu.make_async_copy(
                    image.at[0, pl.ds(low, high - low), columns],
                    img.at[r * padded + c + 1, pl.ds(place, high - low)],
                    load_sem.at[len(loads)],
                )
            )
            loads.append(
                pltpu.make_async_copy(
                    weight.at[0, pl.ds(r * side, side), columns],
                    wgt.at[r * across + c],
                    load_sem.at[len(loads)],
                )
            )
    table_load = pltpu.make_async_copy(tables, tab, load_sem.at[len(loads)])
    for load in loads:
        load.start()
    table_load.start()

    def strip_at(c, j):
        return c if c < chunks - 1 else chunks - 1 + j

    def anchor_copy(c, j, count):
        return pltpu.make_async_copy(
            anchor.at[pl.ds(j, count), pl.ds(c * CHUNK, CHUNK)],
            pre.at[c, pl.ds(j, count)],
            strip_recv.at[strip_at(c, j)],
        )

    @pl.when(sec == 0)
    def _():
        for c in range(chunks - 1):
            anchor_copy(c, 0, blocks).start()
        repeat(blocks, lambda j: anchor_copy(chunks - 1, j, 1).start())
        pre_cor[...] = jnp.zeros(pre_cor.shape, pre_cor.dtype)

    zeros = jnp.zeros(img.shape[1:], img.dtype)
    for r in range(down):
        img[r * padded] = zeros
        img[(r + 1) * padded - 1] = zeros
    for c in range(across):
        img[c + 1, :EDGE] = zeros[:EDGE]
        img[(down - 1) * padded + c + 1, EDGE + side :] = zeros[:EDGE]

    @pl.when(me == 0)
    def _():
        halo[0] = jnp.zeros(halo.shape[1:], halo.dtype)

    @pl.when(me == tiles - 1)
    def _():
        halo[1] = jnp.zeros(halo.shape[1:], halo.dtype)
        for c in range(chunks):
            for ref in (strip, pre):
                ref[c, blocks] = jnp.zeros(ref.shape[2:], ref.dtype)
        for ref in (strip_cor, pre_cor):
            ref[blocks] = jnp.zeros(ref.shape[1:], ref.dtype)

    def remote(src, dst, send, recv, target):
        return pltpu.make_async_remote_copy(
            src_ref=src,
            dst_ref=dst,
            send_sem=send,
            recv_sem=recv,
            device_id=target,
            device_id_type=MESH,
        )

    after_me, before_me = lax.rem(me + 1, tiles), lax.rem(me + tiles - 1, tiles)
    next_sec = lax.rem(sec + 1, sections)
    halo_down = remote(
        image.at[0, pl.ds(th - HALO, HALO)],
        halo.at[0],
        halo_send.at[0],
        halo_recv.at[0],
        (sec, after_me),
    )
    halo_up = remote(
        image.at[0, pl.ds(0, HALO)],
        halo.at[1],
        halo_send.at[1],
        halo_recv.at[1],
        (sec, before_me),
    )

    def onward(c):
        here = pl.ds(0, blocks)
        return remote(
            strip.at[c, here], pre.at[c, here], strip_send.at[c], strip_recv.at[c], (next_sec, me)
        )

    def onward_last(j):
        at = chunks - 1 + j
        return remote(
            strip.at[chunks - 1, j],
            pre.at[chunks - 1, j],
            strip_send.at[at],
            strip_recv.at[at],
            (next_sec, me),
        )

    def own_rim(p):
        return remote(rim_out.at[p], rim_own.at[p], rim_send.at[p], rim_recv.at[p], (sec, before_me))

    def onward_rim(p):
        return remote(
            rim_out.at[p], rim_pre.at[p], next_send.at[p], next_recv.at[p], (next_sec, before_me)
        )

    def anchor_rim(p):
        return remote(
            rim_out.at[pairs + p],
            rim_pre.at[p],
            next_send.at[pairs + 2 + p],
            next_recv.at[p],
            (sec, before_me),
        )

    own_rim_cor = remote(
        strip_cor.at[0], strip_cor.at[blocks], rim_send.at[pairs], rim_recv.at[pairs], (sec, before_me)
    )
    onward_rim_cor = remote(
        strip_cor.at[0],
        pre_cor.at[blocks],
        next_send.at[pairs],
        next_recv.at[pairs],
        (next_sec, before_me),
    )
    onward_cor = remote(
        strip_cor.at[pl.ds(0, blocks)],
        pre_cor.at[pl.ds(0, blocks)],
        next_send.at[pairs + 1],
        next_recv.at[pairs + 1],
        (next_sec, me),
    )

    for load in loads:
        load.wait()

    taps = [taps_ref[0, 0, k] for k in range(25)]
    chips = tiles // 2

    def owner(k):
        chip = lax.rem(me // 2 + 1 + k // 2, chips)
        return chip * 2 + lax.rem(me + 1 + k, 2)

    def live(target, slot):
        return jnp.clip(valid_ref[0, 0, target] - slot, 0, 1).astype(jnp.float32)

    def fill(k, c, ref, place):
        target = owner(k)
        first = pl.multiple_of(c * CHUNK, CHUNK)
        for slot in range(cap):
            source = src_ref[0, 0, slot, target]
            at = source + 2 * lax.div(source, across)
            rows = [
                img[at + n, pl.ds(first, CHUNK + 2 * EDGE)].astype(jnp.float32) for n in range(3)
            ]
            rows = [part[EDGE - 8 : EDGE + CHUNK + 8] for part in rows]
            corrected = lens(rows, taps, 8, CHUNK)
            factor = wgt[source, pl.ds(first, CHUNK)].astype(jnp.float32)
            ref[place, c, slot] = (corrected * factor * live(target, slot)).astype(jnp.bfloat16)

    def block_copy(k, c):
        target = owner(k)
        return remote(
            out_buf.at[target, c],
            in_buf.at[me, c],
            block_send.at[target, c],
            block_recv.at[me, c],
            (sec, target),
        )

    def block_from(k, c):
        source = owner(k)
        return remote(
            out_buf.at[source, c],
            in_buf.at[source, c],
            block_send.at[source, c],
            block_recv.at[source, c],
            (sec, source),
        )

    def cor_copy(k):
        target = owner(k)
        return remote(
            out_cor.at[target], in_cor.at[me], cor_send.at[target], cor_recv.at[me], (sec, target)
        )

    def cor_from(k):
        source = owner(k)
        return remote(
            out_cor.at[source], in_cor.at[source], cor_send.at[source], cor_recv.at[source], (sec, source)
        )

    def pack_rim(ref, p, place):
        low, high = ref[2 * p, 0].astype(jnp.float32), ref[2 * p + 1, 0].astype(jnp.float32)
        lane = lax.broadcasted_iota(jnp.int32, low.shape, 1)
        rim_out[place] = jnp.where(lane < side // 2, low, pltpu.roll(high, side // 2, 1)).astype(
            rim_out.dtype
        )

    def unpack_rim(rim, ref):
        for p in range(pairs):
            packed = rim[p]
            ref[2 * p, blocks] = packed
            ref[2 * p + 1, blocks] = pltpu.roll(packed.astype(jnp.float32), side // 2, 1).astype(
                packed.dtype
            )

    fill(0, 0, out_buf, owner(0))
    after, before = has_next.astype(jnp.int32), has_prev.astype(jnp.int32)
    peers = after * (1 + not_first.astype(jnp.int32)) + before * (1 + not_last.astype(jnp.int32))
    pl.semaphore_wait(barrier, tiles - 1 + peers)

    @pl.when(not_last)
    def _():
        halo_down.start()

    @pl.when(not_first)
    def _():
        halo_up.start()

    block_copy(0, 0).start()

    def send_of(c):
        def step(k):
            fill(k, c, out_buf, owner(k))
            block_copy(k, c).start()

        return step

    pl.loop(1, tiles - 1)(send_of(0))
    fill(tiles - 1, 0, in_buf, me)

    def send_chunk(c):
        pl.loop(0, tiles - 1)(send_of(c))
        fill(tiles - 1, c, in_buf, me)

    pl.loop(1, chunks)(send_chunk)

    @pl.when(not_first)
    def _():
        halo_down.wait_recv()

    @pl.when(not_last)
    def _():
        halo_up.wait_recv()

    row = lax.broadcasted_iota(jnp.int32, (HALO, LANES), 0)

    def halo_terms(n, steps):
        none = jnp.zeros((HALO, LANES), jnp.float32)
        columns = [
            halo[n, :, c * side : (c + 1) * side].astype(jnp.float32) for c in range(across)
        ]
        for c in range(across):
            left = columns[c - 1] if c > 0 else none
            right = columns[c + 1] if c < across - 1 else none
            moved = shifts(left, columns[c], right)
            total = none
            for a, step, kept in steps:
                part = taps[5 * a] * moved[0]
                for b in range(1, 5):
                    part = part + taps[5 * a + b] * moved[b]
                total = total + jnp.where(kept, pltpu.roll(part, step, 0), 0.0)
            yield c, total

    if down > 2:
        for at in range(across, (down - 1) * across):
            cor[at] = jnp.zeros(cor.shape[1:], cor.dtype)
    for c, total in halo_terms(0, ((0, 2, row < 2), (1, 1, row < 1))):
        cor[c] = total * wgt[c, :EDGE].astype(jnp.float32)[:HALO]
    for c, total in halo_terms(1, ((4, 6, row >= 6), (3, 7, row >= 7))):
        at = (down - 1) * across + c
        total = total * wgt[at, side - EDGE :].astype(jnp.float32)[EDGE - HALO :]
        cor[at] = total if down > 1 else cor[at] + total

    def fill_cor(k, ref, place):
        target = owner(k)
        terms = [cor[src_ref[0, 0, slot, target]] * live(target, slot) for slot in range(cap)]
        ref[place] = jnp.concatenate(terms, 0).astype(jnp.bfloat16)

    def send_cor(k):
        fill_cor(k, out_cor, owner(k))
        cor_copy(k).start()

    pl.loop(0, tiles - 1)(send_cor)
    fill_cor(tiles - 1, in_cor, me)

    @pl.when((sec == 0) & not_first)
    def _():
        for c in range(chunks - 1):
            anchor_copy(c, 0, blocks).wait()
        anchor_copy(chunks - 1, 0, 1).wait()
        for p in range(pairs):
            pack_rim(pre, p, pairs + p)
            anchor_rim(p).start()

    def summed(part):
        totals = [None] * blocks
        for t in range(tiles):
            for slot in range(cap):
                value = part(t, slot).astype(jnp.float32)
                place = dst_ref[0, 0, slot, t]
                for j in range(blocks):
                    term = value * (1 - jnp.minimum(jnp.abs(place - j), 1)).astype(jnp.float32)
                    totals[j] = term if totals[j] is None else totals[j] + term
        return [total.astype(jnp.bfloat16) for total in totals]

    def gather_chunk(c):
        repeat(tiles - 1, lambda k: block_from(k, c).wait_recv())
        for j, value in enumerate(summed(lambda t, slot: in_buf[t, c, slot])):
            strip[c, j] = value

    def start_rim(p):
        pack_rim(strip, p, p)

        @pl.when(has_next & not_first)
        def _():
            onward_rim(p).start()

        @pl.when(not_first)
        def _():
            own_rim(p).start()

    for c in range(chunks - 1):
        gather_chunk(c)

        @pl.when(has_next)
        def _():
            onward(c).start()

        if c % 2 == 1:
            start_rim(c // 2)

    repeat(tiles - 1, lambda k: cor_from(k).wait_recv())
    cors = [in_cor[t].astype(jnp.float32) for t in range(tiles)]
    for j, value in enumerate(summed(lambda t, slot: cors[t][slot * HALO : (slot + 1) * HALO])):
        strip_cor[j] = value

    @pl.when(has_next & not_first)
    def _():
        onward_rim_cor.start()

    @pl.when(has_next)
    def _():
        onward_cor.start()

    @pl.when(not_first)
    def _():
        own_rim_cor.start()

    gather_chunk(chunks - 1)
    start_rim(pairs - 1)

    @pl.when(has_next)
    def _():
        repeat(blocks, lambda k: onward_last(blocks - 1 - k).start())

    table_load.wait()
    right_table = tab.at[pl.ds(0, 2 * side)]
    left_table = tab.at[pl.ds(2 * side, 2 * half)]
    inverse_table = tab.at[pl.ds(2 * side + 2 * half, side)]

    def whole(ref, cor_ref, m):
        fix = cor_ref[m].astype(jnp.float32)
        rows = lax.broadcasted_iota(jnp.int32, fix.shape, 0)
        none = jnp.zeros_like(fix)
        top = jnp.concatenate([jnp.where(rows < HALO // 2, fix, 0.0), none], 0)
        bottom = jnp.concatenate([none, jnp.where(rows >= HALO // 2, fix, 0.0)], 0)
        parts = [ref[c, m] for c in range(chunks)]
        first, last = parts[0], parts[-1]
        parts[0] = jnp.concatenate(
            [(first[:16].astype(jnp.float32) + top).astype(first.dtype), first[16:]], 0
        )
        parts[-1] = jnp.concatenate(
            [last[: CHUNK - 16], (last[CHUNK - 16 :].astype(jnp.float32) + bottom).astype(last.dtype)], 0
        )
        return jnp.concatenate(parts, 0)

    def spectra(ref, cor_ref, m):
        block, after = whole(ref, cor_ref, m), whole(ref, cor_ref, m + 1)
        lane = lax.broadcasted_iota(jnp.int32, block.shape, 1)
        shifted = jnp.where(
            lane < side // 2, after.astype(jnp.float32), block.astype(jnp.float32)
        ).astype(block.dtype)
        windows = jnp.concatenate([block, shifted], 0)
        right = jnp.dot(
            windows, right_table[:side], preferred_element_type=jnp.float32
        ).astype(jnp.bfloat16)
        stacked = jnp.concatenate(
            [
                jnp.concatenate([right[:side, :side], right[:side, side:]], 0),
                jnp.concatenate([right[side:, :side], right[side:, side:]], 0),
            ],
            1,
        )
        return jnp.dot(left_table[...], stacked, preferred_element_type=jnp.float32)

    def keep(m):
        spec[m] = spectra(strip, strip_cor, m)

    repeat(blocks - 1, keep)

    @pl.when(not_last)
    def _():
        for p in range(pairs):
            own_rim(p).wait_recv()
        own_rim_cor.wait_recv()
        unpack_rim(rim_own, strip)

    keep(blocks - 1)

    for c in range(chunks - 1):

        @pl.when(has_prev | (me == 0))
        def _():
            onward(c).wait_recv()

    @pl.when(has_prev)
    def _():
        onward_cor.wait_recv()

    @pl.when(has_prev & not_last)
    def _():
        onward_rim_cor.wait_recv()

    @pl.when(not_last)
    def _():
        for p in range(pairs):
            onward_rim(p).wait_recv()
        unpack_rim(rim_pre, pre)

    def correlate(k):
        m = blocks - 1 - k

        @pl.when(has_prev | (me == 0) | (m > 0))
        def _():
            onward_last(m).wait_recv()

        earlier = spectra(pre, pre_cor, m)
        current = spec[m]
        cur_re, cur_im = current[:half], current[half:]
        pre_re, pre_im = earlier[:half], earlier[half:]
        cross_re = cur_re * pre_re + cur_im * pre_im
        cross_im = cur_im * pre_re - cur_re * pre_im
        magnitude = jnp.sqrt(cross_re * cross_re + cross_im * cross_im)
        rows = lax.broadcasted_iota(jnp.int32, (8, side), 0)
        ends = jnp.where(rows < 1, 1.0, 2.0)
        whitened = []
        for n in range(2):
            cols = slice(n * side, (n + 1) * side)
            mag = magnitude[:, cols]
            inner = mag[8:16]
            for at in range(16, half - 8, 8):
                inner = inner + mag[at : at + 8]
            total = 2.0 * inner + ends * (mag[:8] + mag[half - 8 :])
            mean = jnp.sum(total) * (1.0 / (side * side))
            scale = 1.0 / (mag + (0.1 * mean + 1e-06))
            whitened.append(
                jnp.concatenate([cross_re[:, cols] * scale, cross_im[:, cols] * scale], 1)
            )
        whitened = jnp.concatenate(whitened, 0).astype(jnp.bfloat16)
        rows_both = jnp.dot(whitened, right_table[...], preferred_element_type=jnp.float32)
        stacked = jnp.concatenate(
            [
                jnp.concatenate([rows_both[:half, :side], rows_both[:half, side:]], 0),
                jnp.concatenate([rows_both[half:, :side], rows_both[half:, side:]], 0),
            ],
            1,
        ).astype(jnp.bfloat16)
        result = jnp.dot(
            inverse_table[...][:, : 2 * half], stacked, preferred_element_type=jnp.float32
        )
        out[0, 2 * m] = result[:, :side]
        out[0, 2 * m + 1] = result[:, side:]

    repeat(blocks, correlate)

    @pl.when(not_last)
    def _():
        halo_down.wait_send()

    @pl.when(not_first)
    def _():
        halo_up.wait_send()
        for p in range(pairs):
            own_rim(p).wait_send()
        own_rim_cor.wait_send()

    @pl.when(has_next)
    def _():
        for c in range(chunks - 1):
            onward(c).wait_send()
        repeat(blocks, lambda j: onward_last(j).wait_send())
        onward_cor.wait_send()

    @pl.when((sec == 0) & not_first)
    def _():
        for p in range(pairs):
            anchor_rim(p).wait_send()

    @pl.when(has_next & not_first)
    def _():
        for p in range(pairs):
            onward_rim(p).wait_send()
        onward_rim_cor.wait_send()

    def left_here(k):
        for c in range(chunks):
            block_copy(k, c).wait_send()
        cor_copy(k).wait_send()

    repeat(tiles - 1, left_here)


def solution(mesh):
    sections, tiles = mesh.shape["sec"], mesh.shape["tile"]

    def body(image, weight, lens_filter_taps, block_src, block_dst, valid_count, anchor):
        th, tw = image.shape[1:]
        blocks, side = anchor.shape[:2]
        cap = block_src.shape[-1]
        anywhere = pl.BlockSpec(memory_space=pl.ANY)
        bf16 = jnp.bfloat16
        dma = pltpu.SemaphoreType.DMA
        across, down = tw // side, th // side
        chunks, half = side // CHUNK, side // 2 + 8
        pairs = chunks // 2
        tables = dft_tables(side)
        return pl.pallas_call(
            functools.partial(kernel, sections, tiles),
            out_shape=pltpu.VMEM((1, 2 * blocks, side, side), jnp.float32),
            in_specs=[anywhere] * 8,
            out_specs=pl.BlockSpec(memory_space=pltpu.VMEM),
            scratch_shapes=[
                pltpu.SMEM(lens_filter_taps.shape, jnp.float32),
                pltpu.SMEM((1, 1, cap, tiles), jnp.int32),
                pltpu.SMEM((1, 1, cap, tiles), jnp.int32),
                pltpu.SMEM(valid_count.shape, jnp.int32),
                pltpu.VMEM((down * (across + 2), side + 2 * EDGE, side), bf16),
                pltpu.VMEM((down * across, side, side), bf16),
                pltpu.VMEM((2, HALO, tw), bf16),
                pltpu.VMEM((down * across, HALO, side), jnp.float32),
                pltpu.VMEM((tiles, chunks, cap, CHUNK, side), bf16),
                pltpu.VMEM((tiles, chunks, cap, CHUNK, side), bf16),
                pltpu.VMEM((tiles, cap * HALO, side), bf16),
                pltpu.VMEM((tiles, cap * HALO, side), bf16),
                pltpu.VMEM((chunks, blocks + 1, CHUNK, side), bf16),
                pltpu.VMEM((chunks, blocks + 1, CHUNK, side), bf16),
                pltpu.VMEM((blocks + 1, HALO, side), bf16),
                pltpu.VMEM((blocks + 1, HALO, side), bf16),
                pltpu.VMEM((2 * pairs, CHUNK, side), bf16),
                pltpu.VMEM((pairs, CHUNK, side), bf16),
                pltpu.VMEM((pairs, CHUNK, side), bf16),
                pltpu.VMEM((blocks, 2 * half, 2 * side), jnp.float32),
                pltpu.VMEM(tables.shape, bf16),
                dma((2 * down * across + 5,)),
                dma((2,)),
                dma((2,)),
                dma((tiles, chunks)),
                dma((tiles, chunks)),
                dma((tiles,)),
                dma((tiles,)),
                dma((chunks - 1 + blocks,)),
                dma((chunks - 1 + blocks,)),
                dma((pairs + 1,)),
                dma((pairs + 1,)),
                dma((2 * pairs + 2,)),
                dma((pairs + 2,)),
            ],
            compiler_params=pltpu.CompilerParams(collective_id=0, has_side_effects=True),
        )(
            image,
            weight,
            anchor,
            tables,
            lens_filter_taps,
            block_src.transpose(0, 1, 3, 2),
            block_dst.transpose(0, 2, 3, 1),
            valid_count,
        )

    in_specs = (
        P("sec", "tile", None),
        P("sec", "tile", None),
        P("sec", "tile", None),
        P("sec", "tile", None, None),
        P("sec", None, "tile", None),
        P("sec", "tile", None),
        P("tile", None, None),
    )
    out_specs = P("sec", "tile", None, None)
    return jax.shard_map(body, mesh=mesh, in_specs=in_specs, out_specs=out_specs, check_vma=False)
```

time: 16.8 us -> 16.6 us (0.988)
  the two profiles are of different devices: /device:TPU:1 before, /device:TPU:24 now
where the time goes in v1:
time: 16.6 us; the launch traced here: 16.4 us
  Pallas kernels  15.6 us (94%)
  local copies, waits for them, and re-layouts  0.8 us (5%)
    pallas_call x1, Pallas kernels, body(): pl.pallas_call(functools.partial(kernel, sections, tiles), out_shape=pltp...  15.6 us
    unnamed x1, local copies, waits for them, and re-layouts  0.8 us

profile of v1, /device:TPU:24, one launch (start us, length us, event | category | flops | bytes accessed | tf_op | source)
XLA Modules:
  0.0 16.4 jit_solution(2020275503169603293)
XLA Ops:
  0.0 15.6 %shard_map.82 = f32[1,8,128,128]{3,2,1,0:T(8,128)S(1)} custom-call(bf16[1,256,1024]{2,1,0:T(8,128)(2,1)} %image.1, bf16[1,256,1024]{2,1,0:T(8,128)(2,1)} %weight.1, bf16[4,128,128]{2,1,0:T(8,128)(2,1)} %anchor.1, bf16[528,256]{1,0:T(8,128)(2,1)} %constant.2.clone.tables, f32[1,1,25]{2,1,0:T(1,128)} %taps_any.1, s32[1,1,2,4]{3,2,1,0:T(2,128)} %bitcast.2, ...), custom_call_target="tpu_custom_call" | custom-call | tf_op jit(solution)/shard_map/pallas_call | solution.py:709
  15.6 0.8 %copy.10 = f32[1,8,128,128]{3,2,1,0:T(8,128)} copy(f32[1,8,128,128]{3,2,1,0:T(8,128)S(1)} %shard_map.82) | data formatting | bytes 1048576

commit v2 on v1

v2 whole, which is shorter than its diff:
```python
import functools
import math

import jax
import jax.numpy as jnp
import numpy as np
from jax import lax
from jax.experimental import pallas as pl
from jax.experimental.pallas import tpu as pltpu
from jax.sharding import PartitionSpec as P

MESH = pl.DeviceIdType.MESH
EDGE = 8
HALO = 8
CHUNK = 32
LANES = 128


def repeat(count, step):
    if count <= 4:
        for i in range(count):
            step(i)
    else:
        pl.loop(0, count)(step)


def dft_tables(size):
    half = size // 2 + 8
    positions = np.arange(size)
    angle = (positions[:, None] * positions[None, :] % size) * (2.0 * math.pi / size)
    cosine, sine = np.cos(angle), np.sin(angle)
    inverse_right = np.block([[cosine, sine], [-sine, cosine]])
    kept = np.arange(half) <= size // 2
    twice = np.where((np.arange(half) == 0) | (np.arange(half) == size // 2), 1.0, 2.0) * kept
    upper_cos, upper_sin = cosine[:half] * kept[:, None], sine[:half] * kept[:, None]
    forward_left = np.zeros((2 * half, 2 * size))
    forward_left[:, :size] = np.concatenate([upper_cos, upper_sin], 0)
    inverse_left = np.zeros((size, 2 * size))
    inverse_left[:, :half] = cosine[:, :half] * twice / size
    inverse_left[:, half : 2 * half] = -sine[:, :half] * twice / size
    return jnp.asarray(np.concatenate([inverse_right, forward_left, inverse_left], 0), jnp.bfloat16)


def lens(rows, taps, first, count):
    left, middle, right = rows
    lane = lax.broadcasted_iota(jnp.int32, middle.shape, 1)
    shifted = []
    for off in range(-2, 3):
        if off == 0:
            shifted.append(middle)
        elif off > 0:
            mixed = jnp.where(lane < off, right, middle)
            shifted.append(pltpu.roll(mixed, LANES - off, 1))
        else:
            mixed = jnp.where(lane >= LANES + off, left, middle)
            shifted.append(pltpu.roll(mixed, -off, 1))
    total = None
    n = middle.shape[0]
    for a in range(5):
        part = taps[5 * a] * shifted[0]
        for b in range(1, 5):
            part = part + taps[5 * a + b] * shifted[b]
        if a != 2:
            part = pltpu.roll(part, (2 - a) % n, 0)
        part = part[first : first + count]
        total = part if total is None else total + part
    return total


def shifts(left, middle, right):
    lane = lax.broadcasted_iota(jnp.int32, middle.shape, 1)
    shifted = []
    for off in range(-2, 3):
        if off == 0:
            shifted.append(middle)
        elif off > 0:
            shifted.append(pltpu.roll(jnp.where(lane < off, right, middle), LANES - off, 1))
        else:
            shifted.append(pltpu.roll(jnp.where(lane >= LANES + off, left, middle), -off, 1))
    return shifted


def kernel(
    sections,
    tiles,
    image,
    weight,
    anchor,
    tables,
    taps_any,
    src_any,
    dst_any,
    valid_any,
    out,
    taps_ref,
    src_ref,
    dst_ref,
    valid_ref,
    img,
    img_late,
    wgt,
    wgt_late,
    halo,
    cor,
    out_buf,
    in_buf,
    out_cor,
    in_cor,
    strip,
    pre,
    strip_cor,
    pre_cor,
    rim_out,
    rim_anchor,
    rim_own,
    rim_pre,
    spread,
    spec,
    tab,
    places,
    load_sem,
    halo_send,
    halo_recv,
    block_recv,
    strip_recv,
    send_sem,
    recv_sem,
):
    sec = lax.axis_index("sec")
    me = lax.axis_index("tile")
    th, tw = image.shape[1:]
    side = anchor.shape[1]
    chunks, blocks = strip.shape[0], strip.shape[1] - 1
    cap = in_buf.shape[2]
    groups = blocks // 2
    block_send, cor_send, strip_send, strip_cor_send, own_send, next_send, anchor_send = (
        send_sem.at[n] for n in range(7)
    )
    cor_recv, strip_cor_recv, own_recv, next_recv = (recv_sem.at[n] for n in range(4))
    across, down = tw // side, th // side
    padded = across + 2
    half = side // 2 + 8
    pairs = chunks // 2

    barrier = pltpu.get_barrier_semaphore()

    def greet(target):
        pl.semaphore_signal(barrier, inc=1, device_id=target, device_id_type=MESH)

    for k in range(1, tiles):
        greet((sec, lax.rem(me + k, tiles)))
    has_next, has_prev = sec < sections - 1, sec > 0
    not_first, not_last = me > 0, me < tiles - 1

    @pl.when(has_next)
    def _():
        greet((sec + 1, me))

    @pl.when(has_next & not_first)
    def _():
        greet((sec + 1, me - 1))

    @pl.when(has_prev)
    def _():
        greet((sec - 1, me))

    @pl.when(has_prev & not_last)
    def _():
        greet((sec - 1, me + 1))

    loads = []
    for source, ref in (
        (taps_any, taps_ref),
        (src_any, src_ref),
        (dst_any, dst_ref),
        (valid_any, valid_ref),
    ):
        loads.append(pltpu.make_async_copy(source, ref, load_sem.at[len(loads)]))
    early, late = [], []
    early_rows = late_rows = 0
    for r in range(down):
        start, end = r * side - EDGE, (r + 1) * side + EDGE
        top, split = max(0, start), r * side + CHUNK + EDGE
        again, bottom = split - 2 * EDGE, min(th, end)
        early_rows, late_rows = early_rows + split - top, late_rows + bottom - again
        for c in range(across):
            columns = pl.ds(c * side, side)
            at, n = r * padded + c + 1, r * across + c
            early.append(
                pltpu.make_async_copy(
                    image.at[0, pl.ds(top, split - top), columns],
                    img.at[at, pl.ds(top - start, split - top)],
                    load_sem.at[4],
                )
            )
            early.append(
                pltpu.make_async_copy(
                    weight.at[0, pl.ds(r * side, CHUNK), columns], wgt.at[n], load_sem.at[5]
                )
            )
            late.append(
                pltpu.make_async_copy(
                    image.at[0, pl.ds(again, bottom - again), columns],
                    img_late.at[at, pl.ds(0, bottom - again)],
                    load_sem.at[6],
                )
            )
            late.append(
                pltpu.make_async_copy(
                    weight.at[0, pl.ds(r * side + CHUNK, side - CHUNK), columns],
                    wgt_late.at[n],
                    load_sem.at[7],
                )
            )

    def landed(ref, sem):
        pltpu.make_async_copy(ref, ref, sem).wait()

    every = pl.ds(0, down * across)
    table_load = pltpu.make_async_copy(tables, tab, load_sem.at[8])
    for load in loads + early + late:
        load.start()
    table_load.start()

    low_chunks, low_blocks = pl.ds(0, chunks - 1), pl.ds(0, blocks)

    def anchor_copy(c):
        return pltpu.make_async_copy(
            anchor.at[:, pl.ds(c * CHUNK, CHUNK)], pre.at[c, low_blocks], strip_recv.at[0]
        )

    def anchor_last(g):
        return pltpu.make_async_copy(
            anchor.at[pl.ds(2 * g, 2), pl.ds((chunks - 1) * CHUNK, CHUNK)],
            pre.at[chunks - 1, pl.ds(2 * g, 2)],
            strip_recv.at[1 + g],
        )

    @pl.when(sec == 0)
    def _():
        for c in range(chunks - 1):
            anchor_copy(c).start()
        repeat(groups, lambda g: anchor_last(g).start())
        pre_cor[...] = jnp.zeros(pre_cor.shape, pre_cor.dtype)

    for ref in (img, img_late):
        zeros = jnp.zeros(ref.shape[1:], ref.dtype)
        for r in range(down):
            ref[r * padded] = zeros
            ref[(r + 1) * padded - 1] = zeros
    for c in range(across):
        img[c + 1, :EDGE] = zeros[:EDGE]
        img_late[(down - 1) * padded + c + 1, -EDGE:] = zeros[:EDGE]

    @pl.when(me == 0)
    def _():
        halo[0] = jnp.zeros(halo.shape[1:], halo.dtype)

    @pl.when(me == tiles - 1)
    def _():
        halo[1] = jnp.zeros(halo.shape[1:], halo.dtype)
        for c in range(chunks):
            for ref in (strip, pre):
                ref[c, blocks] = jnp.zeros(ref.shape[2:], ref.dtype)

    def remote(src, dst, send, recv, target):
        return pltpu.make_async_remote_copy(
            src_ref=src,
            dst_ref=dst,
            send_sem=send,
            recv_sem=recv,
            device_id=target,
            device_id_type=MESH,
        )

    after_me, before_me = lax.rem(me + 1, tiles), lax.rem(me + tiles - 1, tiles)
    next_sec = lax.rem(sec + 1, sections)
    halo_down = remote(
        image.at[0, pl.ds(th - HALO, HALO)],
        halo.at[0],
        halo_send.at[0],
        halo_recv.at[0],
        (sec, after_me),
    )
    halo_up = remote(
        image.at[0, pl.ds(0, HALO)],
        halo.at[1],
        halo_send.at[1],
        halo_recv.at[1],
        (sec, before_me),
    )

    rim_rows = pairs * CHUNK

    def onward(c):
        return remote(
            strip.at[c, low_blocks],
            pre.at[c, low_blocks],
            strip_send,
            strip_recv.at[0],
            (next_sec, me),
        )

    def onward_last(g):
        here = pl.ds(2 * g, 2)
        return remote(
            strip.at[chunks - 1, here],
            pre.at[chunks - 1, here],
            strip_send,
            strip_recv.at[1 + g],
            (next_sec, me),
        )

    onward_cor = remote(strip_cor, pre_cor, strip_cor_send, strip_cor_recv, (next_sec, me))
    anchor_rim = remote(rim_anchor, rim_pre, anchor_send, next_recv, (sec, before_me))

    def rim_copies(first, count):
        rows = pl.ds(first, count)
        return (
            remote(rim_out.at[rows], rim_own.at[rows], own_send, own_recv, (sec, before_me)),
            remote(rim_out.at[rows], rim_pre.at[rows], next_send, next_recv, (next_sec, before_me)),
        )

    for load in loads:
        load.wait()
    landed(img.at[every, pl.ds(0, early_rows // down)], load_sem.at[4])
    landed(wgt, load_sem.at[5])

    taps = [taps_ref[0, 0, k] for k in range(25)]
    chips = tiles // 2

    def owner(k):
        chip = lax.rem(me // 2 + 1 + k // 2, chips)
        return chip * 2 + lax.rem(me + 1 + k, 2)

    def live(target, slot):
        return jnp.clip(valid_ref[0, 0, target] - slot, 0, 1).astype(jnp.float32)

    def fill(k, c, ref, place, pixels, factors):
        target = owner(k)
        first = 0 if pixels is img else pl.multiple_of((c - 1) * CHUNK, CHUNK)
        for slot in range(cap):
            source = src_ref[0, 0, slot, target]
            at = source + 2 * lax.div(source, across)
            rows = [
                pixels[at + n, pl.ds(first, CHUNK + 2 * EDGE)].astype(jnp.float32) for n in range(3)
            ]
            corrected = lens(rows, taps, EDGE, CHUNK)
            factor = factors[source, pl.ds(first, CHUNK)].astype(jnp.float32)
            ref[c, place, slot] = (corrected * factor * live(target, slot)).astype(jnp.bfloat16)

    def block_copy(k, c):
        target = owner(k)
        return remote(
            out_buf.at[c, target], in_buf.at[c, me], block_send, block_recv.at[c], (sec, target)
        )

    def cor_copy(k):
        target = owner(k)
        return remote(out_cor.at[target], in_cor.at[me], cor_send, cor_recv, (sec, target))

    others = pl.ds(0, tiles - 1)

    def packed_rim(ref, p):
        low, high = ref[2 * p, 0].astype(jnp.float32), ref[2 * p + 1, 0].astype(jnp.float32)
        lane = lax.broadcasted_iota(jnp.int32, low.shape, 1)
        return jnp.where(lane < side // 2, low, pltpu.roll(high, side // 2, 1)).astype(ref.dtype)

    def mended(first, last, fix):
        rows = lax.broadcasted_iota(jnp.int32, fix.shape, 0)
        none = jnp.zeros_like(fix)
        top = jnp.concatenate([jnp.where(rows < HALO // 2, fix, 0.0), none], 0)
        bottom = jnp.concatenate([none, jnp.where(rows >= HALO // 2, fix, 0.0)], 0)
        kind = first.dtype
        first = jnp.concatenate([(first[:16].astype(jnp.float32) + top).astype(kind), first[16:]], 0)
        last = jnp.concatenate(
            [last[: CHUNK - 16], (last[CHUNK - 16 :].astype(jnp.float32) + bottom).astype(kind)], 0
        )
        return first, last

    def unpack_rim(rim, ref):
        parts = []
        for p in range(pairs):
            packed = rim[p * CHUNK : (p + 1) * CHUNK]
            turned = pltpu.roll(packed.astype(jnp.float32), side // 2, 1).astype(packed.dtype)
            parts += [packed, turned]
        fix = rim[rim_rows:].astype(jnp.float32)
        parts[0], parts[-1] = mended(parts[0], parts[-1], fix)
        for c in range(chunks):
            ref[c, blocks] = parts[c]

    fill(0, 0, out_buf, owner(0), img, wgt)
    after, before = has_next.astype(jnp.int32), has_prev.astype(jnp.int32)
    peers = after * (1 + not_first.astype(jnp.int32)) + before * (1 + not_last.astype(jnp.int32))
    pl.semaphore_wait(barrier, tiles - 1 + peers)

    @pl.when(not_last)
    def _():
        halo_down.start()

    @pl.when(not_first)
    def _():
        halo_up.start()

    block_copy(0, 0).start()

    def send_of(c, *held):
        def step(k):
            fill(k, c, out_buf, owner(k), *held)
            block_copy(k, c).start()

        return step

    pl.loop(1, tiles - 1)(send_of(0, img, wgt))
    fill(tiles - 1, 0, in_buf, me, img, wgt)
    landed(img_late.at[every, pl.ds(0, late_rows // down)], load_sem.at[6])
    landed(wgt_late, load_sem.at[7])

    def send_chunk(c):
        pl.loop(0, tiles - 1)(send_of(c, img_late, wgt_late))
        fill(tiles - 1, c, in_buf, me, img_late, wgt_late)

    pl.loop(1, chunks)(send_chunk)

    def place_of(t):
        for slot in range(cap):
            place = dst_ref[0, 0, slot, t]
            for j in range(blocks):
                is_here = (1 - jnp.minimum(jnp.abs(place - j), 1)).astype(jnp.float32)
                places[t, slot * blocks + j] = is_here

    repeat(tiles, place_of)

    @pl.when(not_first)
    def _():
        halo_down.wait_recv()

    @pl.when(not_last)
    def _():
        halo_up.wait_recv()

    row = lax.broadcasted_iota(jnp.int32, (HALO, LANES), 0)

    def halo_terms(n, steps):
        none = jnp.zeros((HALO, LANES), jnp.float32)
        columns = [
            halo[n, :, c * side : (c + 1) * side].astype(jnp.float32) for c in range(across)
        ]
        for c in range(across):
            left = columns[c - 1] if c > 0 else none
            right = columns[c + 1] if c < across - 1 else none
            moved = shifts(left, columns[c], right)
            total = none
            for a, step, kept in steps:
                part = taps[5 * a] * moved[0]
                for b in range(1, 5):
                    part = part + taps[5 * a + b] * moved[b]
                total = total + jnp.where(kept, pltpu.roll(part, step, 0), 0.0)
            yield c, total

    if down > 2:
        for at in range(across, (down - 1) * across):
            cor[at] = jnp.zeros(cor.shape[1:], cor.dtype)
    for c, total in halo_terms(0, ((0, 2, row < 2), (1, 1, row < 1))):
        cor[c] = total * wgt[c, :16].astype(jnp.float32)[:HALO]
    for c, total in halo_terms(1, ((4, 6, row >= 6), (3, 7, row >= 7))):
        at = (down - 1) * across + c
        total = total * wgt_late[at, -16:].astype(jnp.float32)[16 - HALO :]
        cor[at] = total if down > 1 else cor[at] + total

    def fill_cor(k, ref, place):
        target = owner(k)
        terms = [cor[src_ref[0, 0, slot, target]] * live(target, slot) for slot in range(cap)]
        ref[place] = jnp.concatenate(terms, 0).astype(jnp.bfloat16)

    def send_cor(k):
        fill_cor(k, out_cor, owner(k))
        cor_copy(k).start()

    pl.loop(0, tiles - 1)(send_cor)
    fill_cor(tiles - 1, in_cor, me)

    @pl.when((sec == 0) & not_first)
    def _():
        landed(pre.at[low_chunks, low_blocks], strip_recv.at[0])
        landed(pre.at[chunks - 1, pl.ds(0, 2)], strip_recv.at[1])
        for p in range(pairs):
            rim_anchor[p * CHUNK : (p + 1) * CHUNK] = packed_rim(pre, p)
        rim_anchor[rim_rows:] = jnp.zeros((HALO, side), rim_anchor.dtype)
        anchor_rim.start()

    def summed(part):
        totals = [None] * blocks
        for t in range(tiles):
            for slot in range(cap):
                value = part(t, slot).astype(jnp.float32)
                for j in range(blocks):
                    term = value * places[t, slot * blocks + j]
                    totals[j] = term if totals[j] is None else totals[j] + term
        return [total.astype(jnp.bfloat16) for total in totals]

    def gather_chunk(c):
        landed(in_buf.at[c, others], block_recv.at[c])
        for j, value in enumerate(summed(lambda t, slot: in_buf[c, t, slot])):
            strip[c, j] = value

    def start_rim(first, count):
        own, following = rim_copies(first, count)

        @pl.when(has_next & not_first)
        def _():
            following.start()

        @pl.when(not_first)
        def _():
            own.start()

    def send_rim(p):
        rim_out[p * CHUNK : (p + 1) * CHUNK] = packed_rim(strip, p)
        start_rim(p * CHUNK, CHUNK)

    for c in range(chunks - 1):
        gather_chunk(c)

        @pl.when(has_next)
        def _():
            onward(c).start()

        if c % 2 == 1:
            send_rim(c // 2)

    landed(in_cor.at[others], cor_recv)
    cors = [in_cor[t].astype(jnp.float32) for t in range(tiles)]
    for j, value in enumerate(summed(lambda t, slot: cors[t][slot * HALO : (slot + 1) * HALO])):
        strip_cor[j] = value
        if j == 0:
            rim_out[rim_rows:] = value
    start_rim(rim_rows, HALO)

    @pl.when(has_next)
    def _():
        onward_cor.start()

    gather_chunk(chunks - 1)
    send_rim(pairs - 1)

    @pl.when(has_next)
    def _():
        repeat(groups, lambda k: onward_last(groups - 1 - k).start())

    table_load.wait()
    right_table = tab.at[pl.ds(0, 2 * side)]
    left_table = tab.at[pl.ds(2 * side, 2 * half), pl.ds(0, side)]
    inverse_table = tab.at[pl.ds(2 * side + 2 * half, side)]

    def whole(ref, cor_ref, m):
        parts = [ref[c, m] for c in range(chunks)]
        parts[0], parts[-1] = mended(parts[0], parts[-1], cor_ref[m].astype(jnp.float32))
        return jnp.concatenate(parts, 0)

    def over_rows(block):
        return jnp.dot(left_table[...], block, preferred_element_type=jnp.float32)

    def spread_group(ref, cor_ref, g):
        pair = jnp.concatenate([whole(ref, cor_ref, 2 * g), whole(ref, cor_ref, 2 * g + 1)], 1)
        both = over_rows(pair)
        spread[2 * g], spread[2 * g + 1] = both[:, :side], both[:, side:]

    def spread_rim(ref):
        spread[blocks] = over_rows(jnp.concatenate([ref[c, blocks] for c in range(chunks)], 0))

    lane = lax.broadcasted_iota(jnp.int32, (half, side), 1)

    def spectra(g):
        rows = []
        for n in range(2):
            block, after = spread[2 * g + n], spread[2 * g + n + 1]
            parts = [(block[:half], after[:half]), (block[half:], after[half:])]
            rows.append(jnp.concatenate([here for here, _ in parts], 1))
            rows.append(
                jnp.concatenate([jnp.where(lane < side // 2, then, here) for here, then in parts], 1)
            )
        rows = jnp.concatenate(rows, 0).astype(jnp.bfloat16)
        return jnp.dot(rows, right_table[...], preferred_element_type=jnp.float32)

    def keep(g):
        spec[g] = spectra(g)

    repeat(groups, lambda g: spread_group(strip, strip_cor, g))
    repeat(groups - 1, keep)

    @pl.when(not_last)
    def _():
        landed(rim_own, own_recv)
        unpack_rim(rim_own, strip)

    spread_rim(strip)
    keep(groups - 1)

    @pl.when(has_prev | (me == 0))
    def _():
        landed(pre.at[low_chunks, low_blocks], strip_recv.at[0])

    @pl.when(has_prev)
    def _():
        landed(pre_cor, strip_cor_recv)

    @pl.when(not_last)
    def _():
        landed(rim_pre, next_recv)
        unpack_rim(rim_pre, pre)

    spread_rim(pre)

    row = lax.broadcasted_iota(jnp.int32, (8, side), 0)
    ends = jnp.where(row < 1, 1.0, 2.0)

    def correlate(k):
        g = groups - 1 - k

        @pl.when(has_prev | (me == 0) | (g > 0))
        def _():
            landed(pre.at[chunks - 1, pl.ds(2 * g, 2)], strip_recv.at[1 + g])

        spread_group(pre, pre_cor, g)
        earlier, current = spectra(g), spec.at[g]
        whitened = []
        for n in range(4):
            at = slice(n * half, (n + 1) * half)
            cur_re, cur_im = current[at, :side], current[at, side:]
            pre_re, pre_im = earlier[at, :side], earlier[at, side:]
            cross_re = cur_re * pre_re + cur_im * pre_im
            cross_im = cur_re * pre_im - cur_im * pre_re
            mag = jnp.sqrt(cross_re * cross_re + cross_im * cross_im)
            inner = mag[8:16]
            for low in range(16, half - 8, 8):
                inner = inner + mag[low : low + 8]
            total = 2.0 * inner + ends * (mag[:8] + mag[half - 8 :])
            mean = jnp.sum(total) * (1.0 / (side * side))
            scale = 1.0 / (mag + (0.1 * mean + 1e-06))
            whitened.append(jnp.concatenate([cross_re * scale, cross_im * scale], 1))
        whitened = jnp.concatenate(whitened, 0).astype(jnp.bfloat16)
        rows = jnp.dot(whitened, right_table[...], preferred_element_type=jnp.float32)
        for n in range(2):
            stacked = []
            for w in range(2):
                part = rows[(2 * n + w) * half : (2 * n + w + 1) * half]
                stacked.append(jnp.concatenate([part[:, :side], part[:, side:]], 0))
            stacked = jnp.concatenate(stacked, 1).astype(jnp.bfloat16)
            result = jnp.dot(
                inverse_table[...][:, : 2 * half], stacked, preferred_element_type=jnp.float32
            )
            out[0, 4 * g + 2 * n] = result[:, :side]
            out[0, 4 * g + 2 * n + 1] = result[:, side:]

    repeat(groups, correlate)

    @pl.when(not_last)
    def _():
        halo_down.wait_send()

    @pl.when(not_first)
    def _():
        halo_up.wait_send()
        landed(rim_out, own_send)

    @pl.when(has_next)
    def _():
        landed(strip.at[:, low_blocks], strip_send)
        onward_cor.wait_send()

    @pl.when((sec == 0) & not_first)
    def _():
        anchor_rim.wait_send()

    @pl.when(has_next & not_first)
    def _():
        landed(rim_out, next_send)

    landed(out_buf.at[:, others], block_send)
    landed(out_cor.at[others], cor_send)


def solution(mesh):
    sections, tiles = mesh.shape["sec"], mesh.shape["tile"]

    def body(image, weight, lens_filter_taps, block_src, block_dst, valid_count, anchor):
        th, tw = image.shape[1:]
        blocks, side = anchor.shape[:2]
        cap = block_src.shape[-1]
        anywhere = pl.BlockSpec(memory_space=pl.ANY)
        bf16 = jnp.bfloat16
        dma = pltpu.SemaphoreType.DMA
        across, down = tw // side, th // side
        chunks, half = side // CHUNK, side // 2 + 8
        pairs = chunks // 2
        tables = dft_tables(side)
        return pl.pallas_call(
            functools.partial(kernel, sections, tiles),
            out_shape=pltpu.VMEM((1, 2 * blocks, side, side), jnp.float32),
            in_specs=[anywhere] * 8,
            out_specs=pl.BlockSpec(memory_space=pltpu.VMEM),
            scratch_shapes=[
                pltpu.SMEM(lens_filter_taps.shape, jnp.float32),
                pltpu.SMEM((1, 1, cap, tiles), jnp.int32),
                pltpu.SMEM((1, 1, cap, tiles), jnp.int32),
                pltpu.SMEM(valid_count.shape, jnp.int32),
                pltpu.VMEM((down * (across + 2), CHUNK + 2 * EDGE, side), bf16),
                pltpu.VMEM((down * (across + 2), side - CHUNK + 2 * EDGE, side), bf16),
                pltpu.VMEM((down * across, CHUNK, side), bf16),
                pltpu.VMEM((down * across, side - CHUNK, side), bf16),
                pltpu.VMEM((2, HALO, tw), bf16),
                pltpu.VMEM((down * across, HALO, side), jnp.float32),
                pltpu.VMEM((chunks, tiles, cap, CHUNK, side), bf16),
                pltpu.VMEM((chunks, tiles, cap, CHUNK, side), bf16),
                pltpu.VMEM((tiles, cap * HALO, side), bf16),
                pltpu.VMEM((tiles, cap * HALO, side), bf16),
                pltpu.VMEM((chunks, blocks + 1, CHUNK, side), bf16),
                pltpu.VMEM((chunks, blocks + 1, CHUNK, side), bf16),
                pltpu.VMEM((blocks, HALO, side), bf16),
                pltpu.VMEM((blocks, HALO, side), bf16),
                pltpu.VMEM((pairs * CHUNK + HALO, side), bf16),
                pltpu.VMEM((pairs * CHUNK + HALO, side), bf16),
                pltpu.VMEM((pairs * CHUNK + HALO, side), bf16),
                pltpu.VMEM((pairs * CHUNK + HALO, side), bf16),
                pltpu.VMEM((blocks + 1, 2 * half, side), jnp.float32),
                pltpu.VMEM((blocks // 2, 4 * half, 2 * side), jnp.float32),
                pltpu.VMEM(tables.shape, bf16),
                pltpu.SMEM((tiles, cap * blocks), jnp.float32),
                dma((9,)),
                dma((2,)),
                dma((2,)),
                dma((chunks,)),
                dma((1 + blocks // 2,)),
                dma((7,)),
                dma((4,)),
            ],
            compiler_params=pltpu.CompilerParams(collective_id=0, has_side_effects=True),
        )(
            image,
            weight,
            anchor,
            tables,
            lens_filter_taps,
            block_src.transpose(0, 1, 3, 2),
            block_dst.transpose(0, 2, 3, 1),
            valid_count,
        )

    in_specs = (
        P("sec", "tile", None),
        P("sec", "tile", None),
        P("sec", "tile", None),
        P("sec", "tile", None, None),
        P("sec", None, "tile", None),
        P("sec", "tile", None),
        P("tile", None, None),
    )
    out_specs = P("sec", "tile", None, None)
    return jax.shard_map(body, mesh=mesh, in_specs=in_specs, out_specs=out_specs, check_vma=False)
```

time: 16.6 us -> 14.2 us (0.86)
  Pallas kernels: 15.6 us -> 13.3 us
    pallas_call x1, Pallas kernels: 15.6 us -> 13.3 us  [body(): pl.pallas_call(functools.partial(kernel, sections, tiles), out_shape=pltp...]
where the time goes in v2:
time: 14.2 us; the launch traced here: 14.1 us
  Pallas kernels  13.3 us (94%)
  local copies, waits for them, and re-layouts  0.8 us (6%)
    pallas_call x1, Pallas kernels, body(): pl.pallas_call(functools.partial(kernel, sections, tiles), out_shape=pltp...  13.3 us
    unnamed x1, local copies, waits for them, and re-layouts  0.8 us

profile of v2, /device:TPU:24, one launch (start us, length us, event | category | flops | bytes accessed | tf_op | source)
XLA Modules:
  0.0 14.1 jit_solution(3758203789515979776)
XLA Ops:
  0.0 13.3 %shard_map.82 = f32[1,8,128,128]{3,2,1,0:T(8,128)S(1)} custom-call(bf16[1,256,1024]{2,1,0:T(8,128)(2,1)} %image.1, bf16[1,256,1024]{2,1,0:T(8,128)(2,1)} %weight.1, bf16[4,128,128]{2,1,0:T(8,128)(2,1)} %anchor.1, bf16[528,256]{1,0:T(8,128)(2,1)} %constant.2.clone.tables, f32[1,1,25]{2,1,0:T(1,128)} %taps_any.1, s32[1,1,2,4]{3,2,1,0:T(2,128)} %bitcast.2, ...), custom_call_target="tpu_custom_call" | custom-call | tf_op jit(solution)/shard_map/pallas_call | solution.py:698
  13.3 0.8 %copy.10 = f32[1,8,128,128]{3,2,1,0:T(8,128)} copy(f32[1,8,128,128]{3,2,1,0:T(8,128)S(1)} %shard_map.82) | data formatting | bytes 1048576
